TPU v7x, 32 devices: a whole 2x2x4 slice. The times are simulated.
32 devices in a mesh: lon: 8 (over y, x, core), depth: 4 (over z).
Axes of the slice: x: 2, y: 2, z: 4, core: 2. Of those that a mesh axis runs over, the one named last changes fastest.
Arguments:
- innovations: float32 [5, 256, 128, 256], P(None, 'depth', 'lon'), may hold values from -6 to 6
- courant: float32 [3, 256, 128, 256], P(None, 'depth', 'lon'), may hold values from -0.3 to 0.3
- diffusivity: float32 [256, 128, 256], P('depth', 'lon'), may hold values from 0.05 to 0.12
- sea_bricks: int32 [256, 8, 128], P('depth', 'lon'), may hold values 0 or 1
- tile_ranks: int32 [8, 8], P('lon'), may hold values from 16 to 128
- row_factors: bfloat16 [8, 8, 4096, 128], P('lon', None, None, 'depth'), may hold values from -0.09375 to 0.09375
- column_factors: bfloat16 [8, 8, 4096, 128], P('lon', None, None, 'depth'), may hold values from -0.25 to 0.25
Outputs:
- initial_adjoint: float32 [256, 128, 256], P('depth', 'lon')
- gradient: float32 [256, 128, 256], P('depth', 'lon')
All inputs are finite; a program needn't handle non-finite values. No bound on the sum of `sea_bricks` on one device may be relied on, other than what follows from the above.
Results may differ from a plain program's by a relative error of at most 0.0041.
Values may be sent and summed in bfloat16 or wider, within the bound.
No kernel may reach another device: no remote copies, remote signals or barrier semaphores. Data moves between devices by JAX's collectives and lax.ppermute only.
A program may use at most 64 MiB of HBM per device.

v0:
```python
import jax
import jax.numpy as jnp
from jax import lax
from jax.sharding import PartitionSpec as P


def from_behind(value, axis, steps):
    count = lax.axis_size(axis)
    initial, last = (max(0, -steps), min(count, count - steps))
    return lax.ppermute(value, axis, [(source, source + steps) for source in range(initial, last)])


def shifted(block, axis, distance):
    devices = range(lax.axis_size(axis))
    route = [((i - distance) % len(devices), i) for i in devices]
    return lax.ppermute(block, axis, route)


def lat_terms(plus_term, minus_term):
    lower = jnp.pad(plus_term[:, :, :-1], ((0, 0), (0, 0), (1, 0)))
    upper = jnp.pad(minus_term[:, :, 1:], ((0, 0), (0, 0), (0, 1)))
    return lower + upper


def per_device(
    innovations, courant, diffusivity, sea_bricks, tile_ranks, row_factors, column_factors
):
    levels_here, lon_cells, lat_cells = diffusivity.shape
    tile_cols = lon_cells * lat_cells
    blocks_row = tile_ranks.shape[1]
    sea = sea_bricks.astype(jnp.float32)
    sea = jnp.broadcast_to(sea[:, :, :, None], (levels_here, 1, lat_cells // 2, 2)).reshape(
        levels_here, 1, lat_cells
    )
    plus = diffusivity[None] - 0.5 * courant
    minus = diffusivity[None] + 0.5 * courant
    center = 1.0 - 6.0 * diffusivity
    steps_total = innovations.shape[0] - 1
    lam = sea * innovations[steps_total]
    for step in reversed(range(steps_total)):
        plus_term = plus * lam
        minus_term = minus * lam
        below = from_behind(plus_term[0, -1:], "depth", 1)
        above = from_behind(minus_term[0, :1], "depth", -1)
        west = shifted(plus_term[1][:, -1:], "lon", 1)
        east = shifted(minus_term[1][:, :1], "lon", -1)
        out = center * lam
        out = out + jnp.concatenate([below, plus_term[0, :-1]], 0)
        out = out + jnp.concatenate([minus_term[0, 1:], above], 0)
        out = out + jnp.concatenate([west, plus_term[1][:, :-1]], 1)
        out = out + jnp.concatenate([minus_term[1][:, 1:], east], 1)
        lam = sea * (out + lat_terms(plus_term[2], minus_term[2]) + innovations[step])
    lam_half = lam.astype(jnp.bfloat16).reshape(levels_here, tile_cols)
    ranks = tile_ranks[0]
    all_levels = lax.all_gather(lam_half, "depth", axis=0, tiled=True)
    left = row_factors[0]
    width = left.shape[2]
    columns = lax.axis_index("depth") * width + jnp.arange(width, dtype=jnp.int32)
    coeff = jnp.einsum("zt,ktr->kzr", all_levels, left, preferred_element_type=jnp.float32)
    keep = (columns[None, :] < ranks[:, None]).astype(jnp.float32)
    coeff = (coeff * keep[:, None, :]).astype(jnp.bfloat16)
    pieces = []
    for slot in range(blocks_row):
        pieces.append(shifted(coeff[slot], "lon", slot - blocks_row // 2))
    received = jnp.stack(pieces, 0)
    right = column_factors[0]
    gradient = lax.psum_scatter(
        jnp.einsum("kzr,ktr->zt", received, right, preferred_element_type=jnp.float32),
        "depth",
        scatter_dimension=0,
        tiled=True,
    )
    return (lam, gradient.reshape(levels_here, lon_cells, lat_cells))


def solution(mesh):
    placed = (
        P(None, "depth", "lon", None),
        P(None, "depth", "lon", None),
        P("depth", "lon", None),
        P("depth", "lon", None),
        P("lon", None),
        P("lon", None, None, "depth"),
        P("lon", None, None, "depth"),
    )
    return jax.shard_map(
        per_device,
        mesh=mesh,
        in_specs=placed,
        out_specs=(P("depth", "lon", None), P("depth", "lon", None)),
        check_vma=False,
    )
```

profile of v0, /device:TPU:0, one launch (start us, length us, event | category | flops | bytes accessed | tf_op | source)
XLA Modules:
  0.0 223.0 jit_solution(1263880004125982278)
XLA Ops:
  8.4 1.4 multiply_bitcast_fusion
  9.8 2.8 %fusion.8 = (f32[3,64,16,256]{3,2,1,0:T(8,128)S(1)}, f32[3,64,16,256]{3,2,1,0:T(8,128)S(1)}) fusion(f32[3,64,16,256]{3,2,1,0:T(8,128)} %param.8, f32[64,16,256]{2,1,0:T(8,128)S(1)} %multiply_bitcast_fusion, f32[64,16,256]{2,1,0:T(8,128)S(1)} %copy-done.1), kind=kLoop, calls=%fused_computation.11 | loop fusion | flops 3932160 | bytes 11534336 | tf_op jit(solution)/shard_map/mul | solution.py:42
  12.7 5.0 %collective-permute-start = (f32[1,16,256]{2,1,0:T(8,128)S(1)}, f32[1,16,256]{2,1,0:T(8,128)S(1)}, u32[]{:S(2)}, u32[]{:S(2)}) collective-permute-start(f32[1,16,256]{2,1,0:T(8,128)S(1)} %slice_bitcast_fusion.39), channel_id=1, source_target_pairs={{0,1},{1,2},{2,3},{4,5},{5,6},{6,7},{8,9},{9,10},{10,11},{12,13},{... | collective-permute-start | bytes 49160 | tf_op jit(solution)/shard_map/ppermute | solution.py:10
  19.6 2.7 %collective-permute-start.3 = (f32[64,1,256]{2,1,0:T(1,128)S(1)}, f32[64,1,256]{2,1,0:T(1,128)S(1)}, u32[]{:S(2)}, u32[]{:S(2)}) collective-permute-start(f32[64,1,256]{2,1,0:T(1,128)S(1)} %slice.293), channel_id=1, source_target_pairs={{4,0},{8,4},{12,8},{16,12},{20,16},{24,20},{28,24},{0,28},{5,1},{9... | collective-permute-start | bytes 196616 | tf_op jit(solution)/shard_map/ppermute | solution.py:16
  27.6 4.5 %collective-permute-start.4 = (f32[1,16,256]{2,1,0:T(8,128)S(1)}, f32[1,16,256]{2,1,0:T(8,128)S(1)}, u32[]{:S(2)}, u32[]{:S(2)}) collective-permute-start(f32[1,16,256]{2,1,0:T(8,128)S(1)} %slice_bitcast_fusion.37), channel_id=1, source_target_pairs={{0,1},{1,2},{2,3},{4,5},{5,6},{6,7},{8,9},{9,10},{10,11},{12,13},{... | collective-permute-start | bytes 49160 | tf_op jit(solution)/shard_map/ppermute | solution.py:10
  33.5 2.5 %collective-permute-start.7 = (f32[64,1,256]{2,1,0:T(1,128)S(1)}, f32[64,1,256]{2,1,0:T(1,128)S(1)}, u32[]{:S(2)}, u32[]{:S(2)}) collective-permute-start(f32[64,1,256]{2,1,0:T(1,128)S(1)} %slice.307), channel_id=1, source_target_pairs={{4,0},{8,4},{12,8},{16,12},{20,16},{24,20},{28,24},{0,28},{5,1},{9... | collective-permute-start | bytes 196616 | tf_op jit(solution)/shard_map/ppermute | solution.py:16
  37.8 2.8 %collective-permute-done.6 = f32[64,1,256]{2,1,0:T(1,128)S(1)} collective-permute-done((f32[64,1,256]{2,1,0:T(1,128)S(1)}, f32[64,1,256]{2,1,0:T(1,128)S(1)}, u32[]{:S(2)}, u32[]{:S(2)}) %collective-permute-start.6) | collective-permute-done | bytes 65568 | tf_op jit(solution)/shard_map/ppermute | solution.py:16
  43.3 4.3 %collective-permute-start.8 = (f32[1,16,256]{2,1,0:T(8,128)S(1)}, f32[1,16,256]{2,1,0:T(8,128)S(1)}, u32[]{:S(2)}, u32[]{:S(2)}) collective-permute-start(f32[1,16,256]{2,1,0:T(8,128)S(1)} %slice_bitcast_fusion.35), channel_id=1, source_target_pairs={{0,1},{1,2},{2,3},{4,5},{5,6},{6,7},{8,9},{9,10},{10,11},{12,13},{... | collective-permute-start | bytes 49160 | tf_op jit(solution)/shard_map/ppermute | solution.py:10
  50.2 3.1 %collective-permute-done.9 = f32[1,16,256]{2,1,0:T(8,128)S(1)} collective-permute-done((f32[1,16,256]{2,1,0:T(8,128)S(1)}, f32[1,16,256]{2,1,0:T(8,128)S(1)}, u32[]{:S(2)}, u32[]{:S(2)}) %collective-permute-start.9) | collective-permute-done | bytes 16416 | tf_op jit(solution)/shard_map/ppermute | solution.py:10
  57.9 5.4 %collective-permute-start.12 = (f32[1,16,256]{2,1,0:T(8,128)S(1)}, f32[1,16,256]{2,1,0:T(8,128)S(1)}, u32[]{:S(2)}, u32[]{:S(2)}) collective-permute-start(f32[1,16,256]{2,1,0:T(8,128)S(1)} %slice_bitcast_fusion.33), channel_id=1, source_target_pairs={{0,1},{1,2},{2,3},{4,5},{5,6},{6,7},{8,9},{9,10},{10,11},{12,13},{... | collective-permute-start | bytes 49160 | tf_op jit(solution)/shard_map/ppermute | solution.py:10
  63.5 2.7 %collective-permute-start.15 = (f32[64,1,256]{2,1,0:T(1,128)S(1)}, f32[64,1,256]{2,1,0:T(1,128)S(1)}, u32[]{:S(2)}, u32[]{:S(2)}) collective-permute-start(f32[64,1,256]{2,1,0:T(1,128)S(1)} %slice.335), channel_id=1, source_target_pairs={{4,0},{8,4},{12,8},{16,12},{20,16},{24,20},{28,24},{0,28},{5,1},{9... | collective-permute-start | bytes 196616 | tf_op jit(solution)/shard_map/ppermute | solution.py:16
  66.7 1.4 collective-permute-done.14
  68.1 2.2 fusion.35
  71.5 46.6 %all-gather.2.cloned.1.call-done = bf16[256,4096]{1,0:T(8,128)(2,1)} async-done(((bf16[64,4096]{1,0:T(8,128)(2,1)}), bf16[256,4096]{1,0:T(8,128)(2,1)}) %all-gather.2.cloned.1.call-update) | async-done | bytes 2097168 | tf_op jit(solution)/shard_map/all_gather | solution.py:55
  118.1 2.5 %fusion.37 = f32[256,256]{0,1:S(1)} fusion(bf16[256,4096]{1,0:T(8,128)(2,1)} %all-gather.2.cloned.1.call-done, bf16[4096,256]{0,1:T(8,128)(2,1)S(1)} %bitcast.144), kind=kOutput, calls=%fused_computation.97 | convolution fusion | flops 536870912 | bytes 4456448
  120.7 1.5 collective-permute-start.16
  124.5 1.4 collective-permute-start.17
  125.9 1.7 collective-permute-done.17
  127.7 3.4 %collective-permute-start.18 = (bf16[256,32]{0,1:T(8,128)(2,1)S(1)}, bf16[256,32]{0,1:T(8,128)(2,1)S(1)}, u32[]{:S(2)}, u32[]{:S(2)}) collective-permute-start(bf16[256,32]{0,1:T(8,128)(2,1)S(1)} %get-tuple-element.33), channel_id=1, source_target_pairs={{8,0},{12,4},{16,8},{20,12},{24,16},{28,20},{0,24},{4,28},{9,1},{1... | collective-permute-start | bytes 49160 | tf_op jit(solution)/shard_map/ppermute | solution.py:16
  131.1 1.4 collective-permute-done.18
  133.0 1.4 collective-permute-done.19
  134.5 2.7 %convolution_bitcast_fusion = f32[256,4096]{1,0:T(8,128)} fusion(bf16[8,256,32]{1,2,0:T(8,128)(2,1)S(1)} %constant_dynamic-update-slice_fusion, bf16[1,8,4096,32]{2,3,1,0:T(8,128)(2,1)S(1)} %copy-done.3), kind=kOutput, calls=%fused_computation | convolution fusion | flops 536870912 | bytes 6422528 | tf_op jit(solution)/shard_map/kzr,ktr->zt/dot_general | solution.py:68
  137.3 76.4 %reduce-scatter.2.cloned.1.call-done = f32[64,4096]{1,0:T(8,128)} async-done(((f32[256,4096]{1,0:T(8,128)}), f32[64,4096]{1,0:T(8,128)}) %reduce-scatter.2.cloned.1.call-update) | async-done | bytes 1048592 | tf_op jit(solution)/shard_map/reduce_scatter | solution.py:67
  213.7 2.5 %copy.13 = f32[8,8,16,256]{3,2,1,0:T(8,128)} copy(f32[8,8,16,256]{3,1,2,0:T(8,128)} %bitcast.159) | data formatting | bytes 2097152
  (112 shorter events, 26.0 us)
Async XLA Ops:
  7.2 110.9 %all-gather.2.cloned.1.call-start = ((), (), s32[]{:S(2)}) async-start(), calls=%async_computation.1 | async-start | bytes 2621440 | tf_op jit(solution)/shard_map/all_gather | solution.py:55
  12.7 10.3 %collective-permute-start = (f32[1,16,256]{2,1,0:T(8,128)S(1)}, f32[1,16,256]{2,1,0:T(8,128)S(1)}, u32[]{:S(2)}, u32[]{:S(2)}) collective-permute-start(f32[1,16,256]{2,1,0:T(8,128)S(1)} %slice_bitcast_fusion.39), channel_id=1, source_target_pairs={{0,1},{1,2},{2,3},{4,5},{5,6},{6,7},{8,9},{9,10},{10,11},{12,13},{... | collective-permute-start | bytes 49160 | tf_op jit(solution)/shard_map/ppermute | solution.py:10
  17.7 5.6 %collective-permute-start.1 = (f32[1,16,256]{2,1,0:T(8,128)S(1)}, f32[1,16,256]{2,1,0:T(8,128)S(1)}, u32[]{:S(2)}, u32[]{:S(2)}) collective-permute-start(f32[1,16,256]{2,1,0:T(8,128)S(1)} %slice_bitcast_fusion.38), channel_id=1, source_target_pairs={{1,0},{2,1},{3,2},{5,4},{6,5},{7,6},{9,8},{10,9},{11,10},{13,12},{... | collective-permute-start | bytes 49160 | tf_op jit(solution)/shard_map/ppermute | solution.py:10
  19.5 4.6 %collective-permute-start.2 = (f32[64,1,256]{2,1,0:T(1,128)S(1)}, f32[64,1,256]{2,1,0:T(1,128)S(1)}, u32[]{:S(2)}, u32[]{:S(2)}) collective-permute-start(f32[64,1,256]{2,1,0:T(1,128)S(1)} %slice.289), channel_id=1, source_target_pairs={{28,0},{0,4},{4,8},{8,12},{12,16},{16,20},{20,24},{24,28},{29,1},{... | collective-permute-start | bytes 196616 | tf_op jit(solution)/shard_map/ppermute | solution.py:16
  19.6 4.6 %collective-permute-start.3 = (f32[64,1,256]{2,1,0:T(1,128)S(1)}, f32[64,1,256]{2,1,0:T(1,128)S(1)}, u32[]{:S(2)}, u32[]{:S(2)}) collective-permute-start(f32[64,1,256]{2,1,0:T(1,128)S(1)} %slice.293), channel_id=1, source_target_pairs={{4,0},{8,4},{12,8},{16,12},{20,16},{24,20},{28,24},{0,28},{5,1},{9... | collective-permute-start | bytes 196616 | tf_op jit(solution)/shard_map/ppermute | solution.py:16
  27.6 9.0 %collective-permute-start.4 = (f32[1,16,256]{2,1,0:T(8,128)S(1)}, f32[1,16,256]{2,1,0:T(8,128)S(1)}, u32[]{:S(2)}, u32[]{:S(2)}) collective-permute-start(f32[1,16,256]{2,1,0:T(8,128)S(1)} %slice_bitcast_fusion.37), channel_id=1, source_target_pairs={{0,1},{1,2},{2,3},{4,5},{5,6},{6,7},{8,9},{9,10},{10,11},{12,13},{... | collective-permute-start | bytes 49160 | tf_op jit(solution)/shard_map/ppermute | solution.py:10
  32.1 5.6 %collective-permute-start.5 = (f32[1,16,256]{2,1,0:T(8,128)S(1)}, f32[1,16,256]{2,1,0:T(8,128)S(1)}, u32[]{:S(2)}, u32[]{:S(2)}) collective-permute-start(f32[1,16,256]{2,1,0:T(8,128)S(1)} %slice_bitcast_fusion.36), channel_id=1, source_target_pairs={{1,0},{2,1},{3,2},{5,4},{6,5},{7,6},{9,8},{10,9},{11,10},{13,12},{... | collective-permute-start | bytes 49160 | tf_op jit(solution)/shard_map/ppermute | solution.py:10
  33.5 4.4 %collective-permute-start.7 = (f32[64,1,256]{2,1,0:T(1,128)S(1)}, f32[64,1,256]{2,1,0:T(1,128)S(1)}, u32[]{:S(2)}, u32[]{:S(2)}) collective-permute-start(f32[64,1,256]{2,1,0:T(1,128)S(1)} %slice.307), channel_id=1, source_target_pairs={{4,0},{8,4},{12,8},{16,12},{20,16},{24,20},{28,24},{0,28},{5,1},{9... | collective-permute-start | bytes 196616 | tf_op jit(solution)/shard_map/ppermute | solution.py:16
  36.0 4.6 %collective-permute-start.6 = (f32[64,1,256]{2,1,0:T(1,128)S(1)}, f32[64,1,256]{2,1,0:T(1,128)S(1)}, u32[]{:S(2)}, u32[]{:S(2)}) collective-permute-start(f32[64,1,256]{2,1,0:T(1,128)S(1)} %slice.303), channel_id=1, source_target_pairs={{28,0},{0,4},{4,8},{8,12},{12,16},{16,20},{20,24},{24,28},{29,1},{... | collective-permute-start | bytes 196616 | tf_op jit(solution)/shard_map/ppermute | solution.py:16
  43.3 6.8 %collective-permute-start.8 = (f32[1,16,256]{2,1,0:T(8,128)S(1)}, f32[1,16,256]{2,1,0:T(8,128)S(1)}, u32[]{:S(2)}, u32[]{:S(2)}) collective-permute-start(f32[1,16,256]{2,1,0:T(8,128)S(1)} %slice_bitcast_fusion.35), channel_id=1, source_target_pairs={{0,1},{1,2},{2,3},{4,5},{5,6},{6,7},{8,9},{9,10},{10,11},{12,13},{... | collective-permute-start | bytes 49160 | tf_op jit(solution)/shard_map/ppermute | solution.py:10
  47.6 5.6 %collective-permute-start.9 = (f32[1,16,256]{2,1,0:T(8,128)S(1)}, f32[1,16,256]{2,1,0:T(8,128)S(1)}, u32[]{:S(2)}, u32[]{:S(2)}) collective-permute-start(f32[1,16,256]{2,1,0:T(8,128)S(1)} %slice_bitcast_fusion.34), channel_id=1, source_target_pairs={{1,0},{2,1},{3,2},{5,4},{6,5},{7,6},{9,8},{10,9},{11,10},{13,12},{... | collective-permute-start | bytes 49160 | tf_op jit(solution)/shard_map/ppermute | solution.py:10
  49.0 4.3 %collective-permute-start.11 = (f32[64,1,256]{2,1,0:T(1,128)S(1)}, f32[64,1,256]{2,1,0:T(1,128)S(1)}, u32[]{:S(2)}, u32[]{:S(2)}) collective-permute-start(f32[64,1,256]{2,1,0:T(1,128)S(1)} %slice.321), channel_id=1, source_target_pairs={{4,0},{8,4},{12,8},{16,12},{20,16},{24,20},{28,24},{0,28},{5,1},{9... | collective-permute-start | bytes 196616 | tf_op jit(solution)/shard_map/ppermute | solution.py:16
  49.1 4.6 %collective-permute-start.10 = (f32[64,1,256]{2,1,0:T(1,128)S(1)}, f32[64,1,256]{2,1,0:T(1,128)S(1)}, u32[]{:S(2)}, u32[]{:S(2)}) collective-permute-start(f32[64,1,256]{2,1,0:T(1,128)S(1)} %slice.317), channel_id=1, source_target_pairs={{28,0},{0,4},{4,8},{8,12},{12,16},{16,20},{20,24},{24,28},{29,1},{... | collective-permute-start | bytes 196616 | tf_op jit(solution)/shard_map/ppermute | solution.py:16
  56.6 10.1 %collective-permute-start.13 = (f32[1,16,256]{2,1,0:T(8,128)S(1)}, f32[1,16,256]{2,1,0:T(8,128)S(1)}, u32[]{:S(2)}, u32[]{:S(2)}) collective-permute-start(f32[1,16,256]{2,1,0:T(8,128)S(1)} %slice_bitcast_fusion.32), channel_id=1, source_target_pairs={{1,0},{2,1},{3,2},{5,4},{6,5},{7,6},{9,8},{10,9},{11,10},{13,12},{... | collective-permute-start | bytes 49160 | tf_op jit(solution)/shard_map/ppermute | solution.py:10
  57.9 8.8 %collective-permute-start.12 = (f32[1,16,256]{2,1,0:T(8,128)S(1)}, f32[1,16,256]{2,1,0:T(8,128)S(1)}, u32[]{:S(2)}, u32[]{:S(2)}) collective-permute-start(f32[1,16,256]{2,1,0:T(8,128)S(1)} %slice_bitcast_fusion.33), channel_id=1, source_target_pairs={{0,1},{1,2},{2,3},{4,5},{5,6},{6,7},{8,9},{9,10},{10,11},{12,13},{... | collective-permute-start | bytes 49160 | tf_op jit(solution)/shard_map/ppermute | solution.py:10
  63.3 4.8 %collective-permute-start.14 = (f32[64,1,256]{2,1,0:T(1,128)S(1)}, f32[64,1,256]{2,1,0:T(1,128)S(1)}, u32[]{:S(2)}, u32[]{:S(2)}) collective-permute-start(f32[64,1,256]{2,1,0:T(1,128)S(1)} %slice.331), channel_id=1, source_target_pairs={{28,0},{0,4},{4,8},{8,12},{12,16},{16,20},{20,24},{24,28},{29,1},{... | collective-permute-start | bytes 196616 | tf_op jit(solution)/shard_map/ppermute | solution.py:16
  63.5 4.7 %collective-permute-start.15 = (f32[64,1,256]{2,1,0:T(1,128)S(1)}, f32[64,1,256]{2,1,0:T(1,128)S(1)}, u32[]{:S(2)}, u32[]{:S(2)}) collective-permute-start(f32[64,1,256]{2,1,0:T(1,128)S(1)} %slice.335), channel_id=1, source_target_pairs={{4,0},{8,4},{12,8},{16,12},{20,16},{24,20},{28,24},{0,28},{5,1},{9... | collective-permute-start | bytes 196616 | tf_op jit(solution)/shard_map/ppermute | solution.py:16
  71.3 142.3 %reduce-scatter.2.cloned.1.call-start = ((), (), s32[]{:S(2)}) async-start(), calls=%async_computation.2 | async-start | bytes 5242880 | tf_op jit(solution)/shard_map/reduce_scatter | solution.py:67
  120.7 3.8 %collective-permute-start.16 = (bf16[256,32]{0,1:T(8,128)(2,1)S(1)}, bf16[256,32]{0,1:T(8,128)(2,1)S(1)}, u32[]{:S(2)}, u32[]{:S(2)}) collective-permute-start(bf16[256,32]{0,1:T(8,128)(2,1)S(1)} %get-tuple-element.35), channel_id=1, source_target_pairs={{16,0},{20,4},{24,8},{28,12},{0,16},{4,20},{8,24},{12,28},{17,1},{... | collective-permute-start | bytes 49160 | tf_op jit(solution)/shard_map/ppermute | solution.py:16
  122.2 12.3 %collective-permute-start.23 = (bf16[256,32]{0,1:T(8,128)(2,1)S(1)}, bf16[256,32]{0,1:T(8,128)(2,1)S(1)}, u32[]{:S(2)}, u32[]{:S(2)}) collective-permute-start(bf16[256,32]{0,1:T(8,128)(2,1)S(1)} %get-tuple-element.28), channel_id=1, source_target_pairs={{20,0},{24,4},{28,8},{0,12},{4,16},{8,20},{12,24},{16,28},{21,1},{... | collective-permute-start | bytes 49160 | tf_op jit(solution)/shard_map/ppermute | solution.py:16
  122.7 11.8 %collective-permute-start.22 = (bf16[256,32]{0,1:T(8,128)(2,1)S(1)}, bf16[256,32]{0,1:T(8,128)(2,1)S(1)}, u32[]{:S(2)}, u32[]{:S(2)}) collective-permute-start(bf16[256,32]{0,1:T(8,128)(2,1)S(1)} %get-tuple-element.29), channel_id=1, source_target_pairs={{24,0},{28,4},{0,8},{4,12},{8,16},{12,20},{16,24},{20,28},{25,1},{... | collective-permute-start | bytes 49160 | tf_op jit(solution)/shard_map/ppermute | solution.py:16
  123.7 10.8 %collective-permute-start.21 = (bf16[256,32]{0,1:T(8,128)(2,1)S(1)}, bf16[256,32]{0,1:T(8,128)(2,1)S(1)}, u32[]{:S(2)}, u32[]{:S(2)}) collective-permute-start(bf16[256,32]{0,1:T(8,128)(2,1)S(1)} %get-tuple-element.30), channel_id=1, source_target_pairs={{28,0},{0,4},{4,8},{8,12},{12,16},{16,20},{20,24},{24,28},{29,1},{... | collective-permute-start | bytes 49160 | tf_op jit(solution)/shard_map/ppermute | solution.py:16
  124.1 10.4 %collective-permute-start.20 = (bf16[256,32]{0,1:T(8,128)(2,1)S(1)}, bf16[256,32]{0,1:T(8,128)(2,1)S(1)}, u32[]{:S(2)}, u32[]{:S(2)}) collective-permute-start(bf16[256,32]{0,1:T(8,128)(2,1)S(1)} %get-tuple-element.31), channel_id=1, source_target_pairs={{0,0},{4,4},{8,8},{12,12},{16,16},{20,20},{24,24},{28,28},{1,1},{5... | collective-permute-start | bytes 49160 | tf_op jit(solution)/shard_map/ppermute | solution.py:16
  127.7 4.9 %collective-permute-start.18 = (bf16[256,32]{0,1:T(8,128)(2,1)S(1)}, bf16[256,32]{0,1:T(8,128)(2,1)S(1)}, u32[]{:S(2)}, u32[]{:S(2)}) collective-permute-start(bf16[256,32]{0,1:T(8,128)(2,1)S(1)} %get-tuple-element.33), channel_id=1, source_target_pairs={{8,0},{12,4},{16,8},{20,12},{24,16},{28,20},{0,24},{4,28},{9,1},{1... | collective-permute-start | bytes 49160 | tf_op jit(solution)/shard_map/ppermute | solution.py:16
  (9 other events, 150.3 us)
Sparse Core Ops, SparseCore 0:
  71.5 46.5 all-gather.1
  137.4 76.2 reduce-scatter.1
where the time goes:
time: 223 us
  waiting for transfers between devices  138 us (62%)
  starting transfers between devices  41.7 us (19%)
  between operations  14.6 us (7%)
  other arithmetic  14.4 us (6%)
  local copies, waits for them, and re-layouts  8.73 us (4%)
  matrix products  5.16 us (2%)
    reduce_scatter x1, waiting for transfers between devices, per_device(): lax.psum_scatter(jnp.einsum('kzr,ktr->zt', received, right, preferred_ele...  76.4 us
    all_gather x1, waiting for transfers between devices, per_device(): all_levels = lax.all_gather(lam_half, 'depth', axis=0, tiled=True)  46.6 us
    ppermute x8, starting transfers between devices, from_behind(): lax.ppermute(value, axis, [(source, source + steps) for source in range(i...  24.3 us
    ppermute x16, starting transfers between devices, shifted(): return lax.ppermute(block, axis, route)  17.3 us
    ppermute x16, waiting for transfers between devices, shifted(): return lax.ppermute(block, axis, route)  10.8 us
    mul x3, other arithmetic, per_device(): minus_term = minus * lam  4.8 us
    ppermute x8, waiting for transfers between devices, from_behind(): lax.ppermute(value, axis, [(source, source + steps) for source in range(i...  4.56 us
  transfers between devices with their start and end apart: 26, of which 15 were waited for; matrix products, arithmetic and copies ran while one was open for 1% of the time, Pallas kernels for 0%

commit v1 on v0

--- a/solution.py
+++ b/solution.py
@@ -2,6 +2,12 @@
 import jax.numpy as jnp
 from jax import lax
 from jax.sharding import PartitionSpec as P
+
+
+def answer_meshes_in(w_in, along_dim):
+    oldest = list(w_in.shape[1:])
+    oldest[along_dim] *= w_in.shape[0]
+    return jnp.moveaxis(w_in, 0, along_dim).reshape(oldest)
 
 
 def from_behind(value, axis, steps):
@@ -52,7 +58,28 @@
         lam = sea * (out + lat_terms(plus_term[2], minus_term[2]) + innovations[step])
     lam_half = lam.astype(jnp.bfloat16).reshape(levels_here, tile_cols)
     ranks = tile_ranks[0]
-    all_levels = lax.all_gather(lam_half, "depth", axis=0, tiled=True)
+    q_n = lax.axis_size("depth")
+    fields = []
+    for kk in [*range(q_n)]:
+        fields.append((kk, (kk + 1) % q_n))
+    slots = []
+    for dev_j, i0 in fields:
+        slots.append((i0, dev_j))
+    response, n_now = ([], [])
+    for j0 in tuple(range(q_n - 1)):
+        if j0 % 2 == 0:
+            item_now = lax.ppermute(
+                response[-1] if response else lam_half, axis_name="depth", perm=fields
+            )
+            response.append(item_now)
+        else:
+            e_now = lax.ppermute(n_now[-1] if n_now else lam_half, axis_name="depth", perm=slots)
+            n_now.append(e_now)
+    block_next = jnp.stack([*response[::-1], lam_half, *n_now], axis=0)
+    a_now = lax.axis_index("depth")
+    y1 = a_now - len(response)
+    block_next = block_next[(jnp.arange(q_n) - y1) % q_n]
+    all_levels = answer_meshes_in(block_next, 0)
     left = row_factors[0]
     width = left.shape[2]
     columns = lax.axis_index("depth") * width + jnp.arange(width, dtype=jnp.int32)

time: 223 us -> 222 us (level)
  waiting for transfers between devices: 138 us -> 127 us
  local copies, waits for them, and re-layouts: 8.73 us -> 13.8 us
  other arithmetic: 14.4 us -> 17.9 us
    all_gather x1 -> x0, waiting for transfers between devices: 46.6 us -> none  [per_device(): all_levels = lax.all_gather(lam_half, 'depth', axis=0, tiled=True)]
    ppermute x0 -> x3, waiting for transfers between devices: none -> 32.8 us  [the longest x2 23.4 us: per_device(): lax.ppermute(response[-1] if response else lam_half, axis_name='depth', p...]
    ppermute x0 -> x3, starting transfers between devices: none -> 4.01 us  [the longest x2 2.2 us: per_device(): lax.ppermute(response[-1] if response else lam_half, axis_name='depth', p...]
    gather x0 -> x1, local copies, waits for them, and re-layouts: none -> 3.6 us  [per_device(): block_next = block_next[(jnp.arange(q_n) - y1) % q_n]]
    ppermute x16, starting transfers between devices: 17.3 us -> 14.1 us  [shifted(): return lax.ppermute(block, axis, route)]
    another operation x0 -> x1, other arithmetic: none -> 2.96 us  [per_device(): block_next = jnp.stack([*response[::-1], lam_half, *n_now], axis=0)]
  transfers between devices with their start and end apart: 26 -> 28, of which waited for: 15 -> 17; matrix products, arithmetic and copies ran while one was open for 1% -> 2% of each run, Pallas kernels for 0% -> 0%
where the time goes in v1:
time: 222 us; the launch traced here: 221 us
  waiting for transfers between devices  127 us (57%)
  starting transfers between devices  42.5 us (19%)
  other arithmetic  17.9 us (8%)
  between operations  14.6 us (7%)
  local copies, waits for them, and re-layouts  13.8 us (6%)
  matrix products  5.17 us (2%)
    reduce_scatter x1, waiting for transfers between devices, per_device(): lax.psum_scatter(jnp.einsum('kzr,ktr->zt', received, right, preferred_ele...  76.8 us
    ppermute x8, starting transfers between devices, from_behind(): lax.ppermute(value, axis, [(source, source + steps) for source in range(i...  24.3 us
    ppermute x2, waiting for transfers between devices, per_device(): lax.ppermute(response[-1] if response else lam_half, axis_name='depth', p...  23.4 us
    ppermute x16, starting transfers between devices, shifted(): return lax.ppermute(block, axis, route)  14.1 us
    ppermute x16, waiting for transfers between devices, shifted(): return lax.ppermute(block, axis, route)  12.8 us
    ppermute x1, waiting for transfers between devices, per_device(): lax.ppermute(n_now[-1] if n_now else lam_half, axis_name='depth', perm=sl...  9.4 us
    mul x3, other arithmetic, per_device(): minus_term = minus * lam  5.12 us
    ppermute x8, waiting for transfers between devices, from_behind(): lax.ppermute(value, axis, [(source, source + steps) for source in range(i...  4.59 us
  transfers between devices with their start and end apart: 28, of which 17 were waited for; matrix products, arithmetic and copies ran while one was open for 2% of the time, Pallas kernels for 0%

profile of v1, /device:TPU:0, one launch (start us, length us, event | category | flops | bytes accessed | tf_op | source)
XLA Modules:
  0.0 220.9 jit_solution(13519758287987550850)
XLA Ops:
  9.8 2.8 %fusion.8 = (f32[3,64,16,256]{3,2,1,0:T(8,128)S(1)}, f32[3,64,16,256]{3,2,1,0:T(8,128)S(1)}) fusion(f32[3,64,16,256]{3,2,1,0:T(8,128)} %param.8, f32[64,16,256]{2,1,0:T(8,128)S(1)} %multiply_bitcast_fusion, f32[64,16,256]{2,1,0:T(8,128)S(1)} %copy-done.1), kind=kLoop, calls=%fused_computation.13 | loop fusion | flops 3932160 | bytes 11534336 | tf_op jit(solution)/shard_map/mul | solution.py:48
  12.7 5.0 %collective-permute-start = (f32[1,16,256]{2,1,0:T(8,128)S(1)}, f32[1,16,256]{2,1,0:T(8,128)S(1)}, u32[]{:S(2)}, u32[]{:S(2)}) collective-permute-start(f32[1,16,256]{2,1,0:T(8,128)S(1)} %slice_bitcast_fusion.39), channel_id=1, source_target_pairs={{0,1},{1,2},{2,3},{4,5},{5,6},{6,7},{8,9},{9,10},{10,11},{12,13},{... | collective-permute-start | bytes 49160 | tf_op jit(solution)/shard_map/ppermute | solution.py:16
  19.6 2.7 %collective-permute-start.3 = (f32[64,1,256]{2,1,0:T(1,128)S(1)}, f32[64,1,256]{2,1,0:T(1,128)S(1)}, u32[]{:S(2)}, u32[]{:S(2)}) collective-permute-start(f32[64,1,256]{2,1,0:T(1,128)S(1)} %slice.295), channel_id=1, source_target_pairs={{4,0},{8,4},{12,8},{16,12},{20,16},{24,20},{28,24},{0,28},{5,1},{9... | collective-permute-start | bytes 196616 | tf_op jit(solution)/shard_map/ppermute | solution.py:22
  27.7 4.5 %collective-permute-start.4 = (f32[1,16,256]{2,1,0:T(8,128)S(1)}, f32[1,16,256]{2,1,0:T(8,128)S(1)}, u32[]{:S(2)}, u32[]{:S(2)}) collective-permute-start(f32[1,16,256]{2,1,0:T(8,128)S(1)} %slice_bitcast_fusion.37), channel_id=1, source_target_pairs={{0,1},{1,2},{2,3},{4,5},{5,6},{6,7},{8,9},{9,10},{10,11},{12,13},{... | collective-permute-start | bytes 49160 | tf_op jit(solution)/shard_map/ppermute | solution.py:16
  33.6 2.5 %collective-permute-start.7 = (f32[64,1,256]{2,1,0:T(1,128)S(1)}, f32[64,1,256]{2,1,0:T(1,128)S(1)}, u32[]{:S(2)}, u32[]{:S(2)}) collective-permute-start(f32[64,1,256]{2,1,0:T(1,128)S(1)} %slice.309), channel_id=1, source_target_pairs={{4,0},{8,4},{12,8},{16,12},{20,16},{24,20},{28,24},{0,28},{5,1},{9... | collective-permute-start | bytes 196616 | tf_op jit(solution)/shard_map/ppermute | solution.py:22
  38.0 2.8 %collective-permute-done.6 = f32[64,1,256]{2,1,0:T(1,128)S(1)} collective-permute-done((f32[64,1,256]{2,1,0:T(1,128)S(1)}, f32[64,1,256]{2,1,0:T(1,128)S(1)}, u32[]{:S(2)}, u32[]{:S(2)}) %collective-permute-start.6) | collective-permute-done | bytes 65568 | tf_op jit(solution)/shard_map/ppermute | solution.py:22
  43.6 4.3 %collective-permute-start.8 = (f32[1,16,256]{2,1,0:T(8,128)S(1)}, f32[1,16,256]{2,1,0:T(8,128)S(1)}, u32[]{:S(2)}, u32[]{:S(2)}) collective-permute-start(f32[1,16,256]{2,1,0:T(8,128)S(1)} %slice_bitcast_fusion.35), channel_id=1, source_target_pairs={{0,1},{1,2},{2,3},{4,5},{5,6},{6,7},{8,9},{9,10},{10,11},{12,13},{... | collective-permute-start | bytes 49160 | tf_op jit(solution)/shard_map/ppermute | solution.py:16
  50.5 3.1 %collective-permute-done.9 = f32[1,16,256]{2,1,0:T(8,128)S(1)} collective-permute-done((f32[1,16,256]{2,1,0:T(8,128)S(1)}, f32[1,16,256]{2,1,0:T(8,128)S(1)}, u32[]{:S(2)}, u32[]{:S(2)}) %collective-permute-start.9) | collective-permute-done | bytes 16416 | tf_op jit(solution)/shard_map/ppermute | solution.py:16
  58.2 5.4 %collective-permute-start.12 = (f32[1,16,256]{2,1,0:T(8,128)S(1)}, f32[1,16,256]{2,1,0:T(8,128)S(1)}, u32[]{:S(2)}, u32[]{:S(2)}) collective-permute-start(f32[1,16,256]{2,1,0:T(8,128)S(1)} %slice_bitcast_fusion.33), channel_id=1, source_target_pairs={{0,1},{1,2},{2,3},{4,5},{5,6},{6,7},{8,9},{9,10},{10,11},{12,13},{... | collective-permute-start | bytes 49160 | tf_op jit(solution)/shard_map/ppermute | solution.py:16
  63.8 2.7 %collective-permute-start.15 = (f32[64,1,256]{2,1,0:T(1,128)S(1)}, f32[64,1,256]{2,1,0:T(1,128)S(1)}, u32[]{:S(2)}, u32[]{:S(2)}) collective-permute-start(f32[64,1,256]{2,1,0:T(1,128)S(1)} %slice.337), channel_id=1, source_target_pairs={{4,0},{8,4},{12,8},{16,12},{20,16},{24,20},{28,24},{0,28},{5,1},{9... | collective-permute-start | bytes 196616 | tf_op jit(solution)/shard_map/ppermute | solution.py:22
  68.4 2.4 %fusion.37 = (bf16[64,16,256]{2,1,0:T(8,128)(2,1)}, f32[64,16,256]{2,1,0:T(8,128)}) fusion(f32[5,64,16,256]{3,2,1,0:T(8,128)S(1)} %bitcast.153, f32[64,16,255]{2,1,0:T(8,128)S(1)} %slice.341, f32[64,16,255]{2,1,0:T(8,128)S(1)} %bitcast.158, f32[64,1,256]{2,1,0:T(1,128)S(1)} %collective-permute-done.15, f32[64,15,256]{2,1,0:T(8,128)S(1)} %slice.336, ...), kind=kLoop, calls=%fused_computation.105 | loop fusion | flops 4194304 | bytes 11067392 | tf_op jit(solution)/shard_map/convert_element_type | solution.py:59
  72.0 2.1 collective-permute-start.16
  74.1 1.8 collective-permute-start.18
  75.9 13.0 %collective-permute-done.16 = bf16[64,4096]{1,0:T(8,128)(2,1)} collective-permute-done((bf16[64,4096]{1,0:T(8,128)(2,1)S(1)}, bf16[64,4096]{1,0:T(8,128)(2,1)}, u32[]{:S(2)}, u32[]{:S(2)}) %collective-permute-start.16) | collective-permute-done | bytes 524320 | tf_op jit(solution)/shard_map/ppermute | solution.py:71
  90.4 9.4 %collective-permute-done.18 = bf16[64,4096]{1,0:T(8,128)(2,1)} collective-permute-done((bf16[64,4096]{1,0:T(8,128)(2,1)S(1)}, bf16[64,4096]{1,0:T(8,128)(2,1)}, u32[]{:S(2)}, u32[]{:S(2)}) %collective-permute-start.18) | collective-permute-done | bytes 524320 | tf_op jit(solution)/shard_map/ppermute | solution.py:76
  99.8 10.4 %collective-permute-done.17 = bf16[64,4096]{1,0:T(8,128)(2,1)} collective-permute-done((bf16[64,4096]{1,0:T(8,128)(2,1)}, bf16[64,4096]{1,0:T(8,128)(2,1)}, u32[]{:S(2)}, u32[]{:S(2)}) %collective-permute-start.17) | collective-permute-done | bytes 524320 | tf_op jit(solution)/shard_map/ppermute | solution.py:71
  110.2 3.0 %pad_maximum_fusion = bf16[4,64,4096]{2,1,0:T(8,128)(2,1)} fusion(bf16[1,64,4096]{2,1,0:T(8,128)(2,1)} %bitcast.42, bf16[1,64,4096]{2,1,0:T(8,128)(2,1)S(1)} %stack_reshape.3, bf16[1,64,4096]{2,1,0:T(8,128)(2,1)} %bitcast.41, bf16[1,64,4096]{2,1,0:T(8,128)(2,1)} %bitcast.40), kind=kLoop, calls=%fused_computation.4 | loop fusion | flops 3145728 | bytes 4194304 | tf_op jit(solution)/shard_map/stack | solution.py:78
  113.2 3.6 %gather_fusion = bf16[4,64,4096]{2,1,0:T(8,128)(2,1)} fusion(bf16[4,64,4096]{2,1,0:T(8,128)(2,1)} %pad_maximum_fusion, s32[1024]{0:T(1024)S(1)} %pad_clamp_fusion), kind=kCustom, calls=%fused_computation | custom fusion | bytes 4194320 | tf_op jit(solution)/shard_map/gather | solution.py:81
  116.8 2.5 %fusion.39 = f32[256,256]{0,1:S(1)} fusion(bf16[256,4096]{1,0:T(8,128)(2,1)} %bitcast.151, bf16[4096,256]{0,1:T(8,128)(2,1)S(1)} %bitcast.150), kind=kOutput, calls=%fused_computation.106 | convolution fusion | flops 536870912 | bytes 4456448
  124.1 2.3 %collective-permute-done.20 = bf16[256,32]{0,1:T(8,128)(2,1)S(1)} collective-permute-done((bf16[256,32]{0,1:T(8,128)(2,1)S(1)}, bf16[256,32]{0,1:T(8,128)(2,1)S(1)}, u32[]{:S(2)}, u32[]{:S(2)}) %collective-permute-start.20) | collective-permute-done | bytes 16416 | tf_op jit(solution)/shard_map/ppermute | solution.py:22
  126.4 2.0 collective-permute-start.21
  132.1 2.7 %convolution_bitcast_fusion = f32[256,4096]{1,0:T(8,128)} fusion(bf16[8,256,32]{1,2,0:T(8,128)(2,1)S(1)} %constant_dynamic-update-slice_fusion, bf16[1,8,4096,32]{2,3,1,0:T(8,128)(2,1)S(1)} %copy-done.3), kind=kOutput, calls=%fused_computation.1 | convolution fusion | flops 536870912 | bytes 6422528 | tf_op jit(solution)/shard_map/kzr,ktr->zt/dot_general | solution.py:95
  134.8 76.8 %reduce-scatter.2.cloned.1.call-done = f32[64,4096]{1,0:T(8,128)} async-done(((f32[256,4096]{1,0:T(8,128)}), f32[64,4096]{1,0:T(8,128)}) %reduce-scatter.2.cloned.1.call-update) | async-done | bytes 1048592 | tf_op jit(solution)/shard_map/reduce_scatter | solution.py:94
  211.6 2.5 %copy.13 = f32[8,8,16,256]{3,2,1,0:T(8,128)} copy(f32[8,8,16,256]{3,1,2,0:T(8,128)} %bitcast.164) | data formatting | bytes 2097152
  (120 shorter events, 36.4 us)
Async XLA Ops:
  7.2 204.4 %reduce-scatter.2.cloned.1.call-start = ((), (), s32[]{:S(2)}) async-start(), calls=%async_computation.1 | async-start | bytes 5242880 | tf_op jit(solution)/shard_map/reduce_scatter | solution.py:94
  12.7 10.2 %collective-permute-start = (f32[1,16,256]{2,1,0:T(8,128)S(1)}, f32[1,16,256]{2,1,0:T(8,128)S(1)}, u32[]{:S(2)}, u32[]{:S(2)}) collective-permute-start(f32[1,16,256]{2,1,0:T(8,128)S(1)} %slice_bitcast_fusion.39), channel_id=1, source_target_pairs={{0,1},{1,2},{2,3},{4,5},{5,6},{6,7},{8,9},{9,10},{10,11},{12,13},{... | collective-permute-start | bytes 49160 | tf_op jit(solution)/shard_map/ppermute | solution.py:16
  17.7 5.6 %collective-permute-start.1 = (f32[1,16,256]{2,1,0:T(8,128)S(1)}, f32[1,16,256]{2,1,0:T(8,128)S(1)}, u32[]{:S(2)}, u32[]{:S(2)}) collective-permute-start(f32[1,16,256]{2,1,0:T(8,128)S(1)} %slice_bitcast_fusion.38), channel_id=1, source_target_pairs={{1,0},{2,1},{3,2},{5,4},{6,5},{7,6},{9,8},{10,9},{11,10},{13,12},{... | collective-permute-start | bytes 49160 | tf_op jit(solution)/shard_map/ppermute | solution.py:16
  19.5 4.6 %collective-permute-start.2 = (f32[64,1,256]{2,1,0:T(1,128)S(1)}, f32[64,1,256]{2,1,0:T(1,128)S(1)}, u32[]{:S(2)}, u32[]{:S(2)}) collective-permute-start(f32[64,1,256]{2,1,0:T(1,128)S(1)} %slice.291), channel_id=1, source_target_pairs={{28,0},{0,4},{4,8},{8,12},{12,16},{16,20},{20,24},{24,28},{29,1},{... | collective-permute-start | bytes 196616 | tf_op jit(solution)/shard_map/ppermute | solution.py:22
  19.6 4.6 %collective-permute-start.3 = (f32[64,1,256]{2,1,0:T(1,128)S(1)}, f32[64,1,256]{2,1,0:T(1,128)S(1)}, u32[]{:S(2)}, u32[]{:S(2)}) collective-permute-start(f32[64,1,256]{2,1,0:T(1,128)S(1)} %slice.295), channel_id=1, source_target_pairs={{4,0},{8,4},{12,8},{16,12},{20,16},{24,20},{28,24},{0,28},{5,1},{9... | collective-permute-start | bytes 196616 | tf_op jit(solution)/shard_map/ppermute | solution.py:22
  27.7 9.0 %collective-permute-start.4 = (f32[1,16,256]{2,1,0:T(8,128)S(1)}, f32[1,16,256]{2,1,0:T(8,128)S(1)}, u32[]{:S(2)}, u32[]{:S(2)}) collective-permute-start(f32[1,16,256]{2,1,0:T(8,128)S(1)} %slice_bitcast_fusion.37), channel_id=1, source_target_pairs={{0,1},{1,2},{2,3},{4,5},{5,6},{6,7},{8,9},{9,10},{10,11},{12,13},{... | collective-permute-start | bytes 49160 | tf_op jit(solution)/shard_map/ppermute | solution.py:16
  32.3 5.6 %collective-permute-start.5 = (f32[1,16,256]{2,1,0:T(8,128)S(1)}, f32[1,16,256]{2,1,0:T(8,128)S(1)}, u32[]{:S(2)}, u32[]{:S(2)}) collective-permute-start(f32[1,16,256]{2,1,0:T(8,128)S(1)} %slice_bitcast_fusion.36), channel_id=1, source_target_pairs={{1,0},{2,1},{3,2},{5,4},{6,5},{7,6},{9,8},{10,9},{11,10},{13,12},{... | collective-permute-start | bytes 49160 | tf_op jit(solution)/shard_map/ppermute | solution.py:16
  33.6 4.4 %collective-permute-start.7 = (f32[64,1,256]{2,1,0:T(1,128)S(1)}, f32[64,1,256]{2,1,0:T(1,128)S(1)}, u32[]{:S(2)}, u32[]{:S(2)}) collective-permute-start(f32[64,1,256]{2,1,0:T(1,128)S(1)} %slice.309), channel_id=1, source_target_pairs={{4,0},{8,4},{12,8},{16,12},{20,16},{24,20},{28,24},{0,28},{5,1},{9... | collective-permute-start | bytes 196616 | tf_op jit(solution)/shard_map/ppermute | solution.py:22
  36.1 4.6 %collective-permute-start.6 = (f32[64,1,256]{2,1,0:T(1,128)S(1)}, f32[64,1,256]{2,1,0:T(1,128)S(1)}, u32[]{:S(2)}, u32[]{:S(2)}) collective-permute-start(f32[64,1,256]{2,1,0:T(1,128)S(1)} %slice.305), channel_id=1, source_target_pairs={{28,0},{0,4},{4,8},{8,12},{12,16},{16,20},{20,24},{24,28},{29,1},{... | collective-permute-start | bytes 196616 | tf_op jit(solution)/shard_map/ppermute | solution.py:22
  43.6 6.8 %collective-permute-start.8 = (f32[1,16,256]{2,1,0:T(8,128)S(1)}, f32[1,16,256]{2,1,0:T(8,128)S(1)}, u32[]{:S(2)}, u32[]{:S(2)}) collective-permute-start(f32[1,16,256]{2,1,0:T(8,128)S(1)} %slice_bitcast_fusion.35), channel_id=1, source_target_pairs={{0,1},{1,2},{2,3},{4,5},{5,6},{6,7},{8,9},{9,10},{10,11},{12,13},{... | collective-permute-start | bytes 49160 | tf_op jit(solution)/shard_map/ppermute | solution.py:16
  47.9 5.6 %collective-permute-start.9 = (f32[1,16,256]{2,1,0:T(8,128)S(1)}, f32[1,16,256]{2,1,0:T(8,128)S(1)}, u32[]{:S(2)}, u32[]{:S(2)}) collective-permute-start(f32[1,16,256]{2,1,0:T(8,128)S(1)} %slice_bitcast_fusion.34), channel_id=1, source_target_pairs={{1,0},{2,1},{3,2},{5,4},{6,5},{7,6},{9,8},{10,9},{11,10},{13,12},{... | collective-permute-start | bytes 49160 | tf_op jit(solution)/shard_map/ppermute | solution.py:16
  49.3 4.3 %collective-permute-start.11 = (f32[64,1,256]{2,1,0:T(1,128)S(1)}, f32[64,1,256]{2,1,0:T(1,128)S(1)}, u32[]{:S(2)}, u32[]{:S(2)}) collective-permute-start(f32[64,1,256]{2,1,0:T(1,128)S(1)} %slice.323), channel_id=1, source_target_pairs={{4,0},{8,4},{12,8},{16,12},{20,16},{24,20},{28,24},{0,28},{5,1},{9... | collective-permute-start | bytes 196616 | tf_op jit(solution)/shard_map/ppermute | solution.py:22
  49.4 4.6 %collective-permute-start.10 = (f32[64,1,256]{2,1,0:T(1,128)S(1)}, f32[64,1,256]{2,1,0:T(1,128)S(1)}, u32[]{:S(2)}, u32[]{:S(2)}) collective-permute-start(f32[64,1,256]{2,1,0:T(1,128)S(1)} %slice.319), channel_id=1, source_target_pairs={{28,0},{0,4},{4,8},{8,12},{12,16},{16,20},{20,24},{24,28},{29,1},{... | collective-permute-start | bytes 196616 | tf_op jit(solution)/shard_map/ppermute | solution.py:22
  56.9 10.1 %collective-permute-start.13 = (f32[1,16,256]{2,1,0:T(8,128)S(1)}, f32[1,16,256]{2,1,0:T(8,128)S(1)}, u32[]{:S(2)}, u32[]{:S(2)}) collective-permute-start(f32[1,16,256]{2,1,0:T(8,128)S(1)} %slice_bitcast_fusion.32), channel_id=1, source_target_pairs={{1,0},{2,1},{3,2},{5,4},{6,5},{7,6},{9,8},{10,9},{11,10},{13,12},{... | collective-permute-start | bytes 49160 | tf_op jit(solution)/shard_map/ppermute | solution.py:16
  58.2 8.8 %collective-permute-start.12 = (f32[1,16,256]{2,1,0:T(8,128)S(1)}, f32[1,16,256]{2,1,0:T(8,128)S(1)}, u32[]{:S(2)}, u32[]{:S(2)}) collective-permute-start(f32[1,16,256]{2,1,0:T(8,128)S(1)} %slice_bitcast_fusion.33), channel_id=1, source_target_pairs={{0,1},{1,2},{2,3},{4,5},{5,6},{6,7},{8,9},{9,10},{10,11},{12,13},{... | collective-permute-start | bytes 49160 | tf_op jit(solution)/shard_map/ppermute | solution.py:16
  63.6 4.8 %collective-permute-start.14 = (f32[64,1,256]{2,1,0:T(1,128)S(1)}, f32[64,1,256]{2,1,0:T(1,128)S(1)}, u32[]{:S(2)}, u32[]{:S(2)}) collective-permute-start(f32[64,1,256]{2,1,0:T(1,128)S(1)} %slice.333), channel_id=1, source_target_pairs={{28,0},{0,4},{4,8},{8,12},{12,16},{16,20},{20,24},{24,28},{29,1},{... | collective-permute-start | bytes 196616 | tf_op jit(solution)/shard_map/ppermute | solution.py:22
  63.8 4.7 %collective-permute-start.15 = (f32[64,1,256]{2,1,0:T(1,128)S(1)}, f32[64,1,256]{2,1,0:T(1,128)S(1)}, u32[]{:S(2)}, u32[]{:S(2)}) collective-permute-start(f32[64,1,256]{2,1,0:T(1,128)S(1)} %slice.337), channel_id=1, source_target_pairs={{4,0},{8,4},{12,8},{16,12},{20,16},{24,20},{28,24},{0,28},{5,1},{9... | collective-permute-start | bytes 196616 | tf_op jit(solution)/shard_map/ppermute | solution.py:22
  72.0 16.8 %collective-permute-start.16 = (bf16[64,4096]{1,0:T(8,128)(2,1)S(1)}, bf16[64,4096]{1,0:T(8,128)(2,1)}, u32[]{:S(2)}, u32[]{:S(2)}) collective-permute-start(bf16[64,4096]{1,0:T(8,128)(2,1)S(1)} %bitcast.166), channel_id=1, source_target_pairs={{0,1},{1,2},{2,3},{3,0},{4,5},{5,6},{6,7},{7,4},{8,9},{9,10},{10,1... | collective-permute-start | bytes 1572872 | tf_op jit(solution)/shard_map/ppermute | solution.py:71
  74.1 25.7 %collective-permute-start.18 = (bf16[64,4096]{1,0:T(8,128)(2,1)S(1)}, bf16[64,4096]{1,0:T(8,128)(2,1)}, u32[]{:S(2)}, u32[]{:S(2)}) collective-permute-start(bf16[64,4096]{1,0:T(8,128)(2,1)S(1)} %bitcast.167), channel_id=1, source_target_pairs={{1,0},{2,1},{3,2},{0,3},{5,4},{6,5},{7,6},{4,7},{9,8},{10,9},{11,1... | collective-permute-start | bytes 1572872 | tf_op jit(solution)/shard_map/ppermute | solution.py:76
  88.9 21.3 %collective-permute-start.17 = (bf16[64,4096]{1,0:T(8,128)(2,1)}, bf16[64,4096]{1,0:T(8,128)(2,1)}, u32[]{:S(2)}, u32[]{:S(2)}) collective-permute-start(bf16[64,4096]{1,0:T(8,128)(2,1)} %collective-permute-done.16), channel_id=1, source_target_pairs={{0,1},{1,2},{2,3},{3,0},{4,5},{5,6},{6,7},{7,4},{8,9},{9,10},{10,1... | collective-permute-start | bytes 1572872 | tf_op jit(solution)/shard_map/ppermute | solution.py:71
  120.9 11.2 %collective-permute-start.26 = (bf16[256,32]{0,1:T(8,128)(2,1)S(1)}, bf16[256,32]{0,1:T(8,128)(2,1)S(1)}, u32[]{:S(2)}, u32[]{:S(2)}) collective-permute-start(bf16[256,32]{0,1:T(8,128)(2,1)S(1)} %get-tuple-element.28), channel_id=1, source_target_pairs={{20,0},{24,4},{28,8},{0,12},{4,16},{8,20},{12,24},{16,28},{21,1},{... | collective-permute-start | bytes 49160 | tf_op jit(solution)/shard_map/ppermute | solution.py:22
  120.9 11.2 %collective-permute-start.25 = (bf16[256,32]{0,1:T(8,128)(2,1)S(1)}, bf16[256,32]{0,1:T(8,128)(2,1)S(1)}, u32[]{:S(2)}, u32[]{:S(2)}) collective-permute-start(bf16[256,32]{0,1:T(8,128)(2,1)S(1)} %get-tuple-element.29), channel_id=1, source_target_pairs={{24,0},{28,4},{0,8},{4,12},{8,16},{12,20},{16,24},{20,28},{25,1},{... | collective-permute-start | bytes 49160 | tf_op jit(solution)/shard_map/ppermute | solution.py:22
  121.3 10.8 %collective-permute-start.24 = (bf16[256,32]{0,1:T(8,128)(2,1)S(1)}, bf16[256,32]{0,1:T(8,128)(2,1)S(1)}, u32[]{:S(2)}, u32[]{:S(2)}) collective-permute-start(bf16[256,32]{0,1:T(8,128)(2,1)S(1)} %get-tuple-element.30), channel_id=1, source_target_pairs={{28,0},{0,4},{4,8},{8,12},{12,16},{16,20},{20,24},{24,28},{29,1},{... | collective-permute-start | bytes 49160 | tf_op jit(solution)/shard_map/ppermute | solution.py:22
  121.6 10.4 %collective-permute-start.23 = (bf16[256,32]{0,1:T(8,128)(2,1)S(1)}, bf16[256,32]{0,1:T(8,128)(2,1)S(1)}, u32[]{:S(2)}, u32[]{:S(2)}) collective-permute-start(bf16[256,32]{0,1:T(8,128)(2,1)S(1)} %get-tuple-element.31), channel_id=1, source_target_pairs={{0,0},{4,4},{8,8},{12,12},{16,16},{20,20},{24,24},{28,28},{1,1},{5... | collective-permute-start | bytes 49160 | tf_op jit(solution)/shard_map/ppermute | solution.py:22
  (11 other events, 172.8 us)
Sparse Core Ops, SparseCore 0:
  134.9 76.5 reduce-scatter.1
